TPU v7x, 32 devices: a whole 2x2x4 slice. The times are simulated.
32 devices in a mesh: row: 16 (over z, y, core), col: 2 (over x).
Axes of the slice: x: 2, y: 2, z: 4, core: 2. Of those that a mesh axis runs over, the one named last changes fastest.
Arguments:
- start_block: float32 [4096, 256], P(('row', 'col')), may hold values from -6 to 6
- tiles: bfloat16 [16, 2, 14, 128, 128], P('row', 'col'), may hold values from -0.125 to 0.125
- tile_rows: int32 [16, 2, 14], P('row', 'col'), may hold values from -1 to 31, as said below
- tile_cols: int32 [16, 2, 14], P('row', 'col'), may hold values from -1 to 31, as said below
- bounds: float32 [3], replicated, may hold values from -2.6 to 2.6, as said below
Outputs:
- filtered: float32 [4096, 256], P(('row', 'col'))
Inputs may be any that keep to these rules, and one draw needn't show every extreme that they name: Vector rows form blocks of 128 rows, one block a device, in row+col order. On the device at grid row r and grid column c, a live slot names a block row held by one of the devices (r, any column) and a block column held by one of the devices (any row, c). Live slots come first; each device has 1 to 14 live slots, and one device has exactly 14 in every draw. No block position is named twice, and the mirror of a named position is never named unless it lies on the diagonal. tile_rows and tile_cols are -1 together. `tile_cols`: same slots as tile_rows. bounds[0] < bounds[1] < bounds[2].
All inputs are finite; a program needn't handle non-finite values.
Results may differ from a plain program's by a relative error of at most 0.0042.
Values may be sent and summed in bfloat16 or wider, within the bound.
A program may use at most 64 MiB of HBM per device.

v0:
```python
import functools

import jax
import jax.numpy as jnp
from jax import lax
from jax.experimental import pallas as pl
from jax.experimental.pallas import tpu as pltpu
from jax.sharding import PartitionSpec as P

DEGREE = 4
CHAINS = 2
LAG = 0
MESH = pl.DeviceIdType.MESH


def kernel(
    far, near, slots, tile, width,
    rows_ref, cols_ref, bounds_ref, start_ref, tiles_ref, out_ref,
    placed, owned, mirror, window, diagonal, low, partial, arrived, mine, state,
    tile_send, tile_recv, low_send, low_recv, part_send, part_recv,
):
    chips = far // 2
    tall = far // 4
    count = far * near
    cut = width // CHAINS
    row = lax.axis_index("row")
    col = lax.axis_index("col")
    me = row * near + col
    core = row % 2
    mid = row // 2 % 2
    high = row // 4

    def spot(high_at, mid_at, core_at):
        return core_at * chips + high_at * 2 + mid_at

    def row_of(high_at, mid_at, core_at):
        return (high_at * 2 + mid_at) * 2 + core_at

    own_spot = spot(high, mid, core)

    barrier = pltpu.get_barrier_semaphore()

    def greet(step, carry):
        other = (me + step) % count
        pl.semaphore_signal(
            barrier, inc=1, device_id=(other // near, other % near), device_id_type=MESH
        )
        return carry

    lax.fori_loop(1, count, greet, 0)

    line = (1, cut)
    lowest = jnp.full(line, bounds_ref[0], jnp.float32)
    lower = jnp.full(line, bounds_ref[1], jnp.float32)
    upper = jnp.full(line, bounds_ref[2], jnp.float32)
    half_width = (upper - lower) * 0.5
    center = (upper + lower) * 0.5
    sigma_one = half_width / (lowest - center)

    def columns(chain):
        return slice(chain * cut, (chain + 1) * cut)

    for chain in range(CHAINS):
        low[0, chain, own_spot] = start_ref[:, columns(chain)].astype(jnp.bfloat16)

    for slot in range(slots):
        placed[slot] = tiles_ref[slot]
    placed[slots] = jnp.zeros((tile, tile), jnp.bfloat16)
    places = []
    for slot in range(slots):
        glob_row = rows_ref[slot]
        glob_col = cols_ref[slot]
        place = (glob_col // near) * near + (glob_row - row * near)
        places.append(jnp.where(glob_row >= 0, place, -1))

    def put(position, carry):
        chosen = jnp.int32(slots)
        for slot in range(slots):
            chosen = jnp.where(places[slot] == position, slot, chosen)
        owned[position] = placed[chosen]
        return carry

    lax.fori_loop(0, count, put, 0)
    diagonal[...] = owned[me]
    mirror[me] = diagonal[...]
    owned[me] = jnp.zeros((tile, tile), jnp.bfloat16)

    pl.semaphore_wait(barrier, count - 1)

    flip = high >= tall // 2
    near_end = jnp.where(flip, tall - 1 - high, high)

    def along(position):
        return jnp.where(flip, tall - 1 - position, position)

    def ranked(index):
        return index + jnp.where(index >= near_end, 1, 0)

    def send_low(step, chain, place, target_row):
        pltpu.make_async_remote_copy(
            src_ref=low.at[step, chain, place],
            dst_ref=low.at[step, chain, place],
            send_sem=low_send.at[step, chain],
            recv_sem=low_recv.at[step, chain, place],
            device_id=(target_row, col),
            device_id_type=MESH,
        ).start()

    def await_low(step, chain, place):
        here = low.at[step, chain, place]
        pltpu.make_async_copy(here, here, low_recv.at[step, chain, place]).wait()

    def begin(step, chain):
        send_low(step, chain, own_spot, row_of(high, 1 - mid, core))
        for index in range(tall - 1):
            send_low(step, chain, own_spot, row_of(along(ranked(index)), mid, core))
        send_low(step, chain, own_spot, row_of(high, mid, 1 - core))

    def forward_line(step, chain):
        for index in range(tall - 1):
            place = spot(along(ranked(index)), mid, core)
            await_low(step, chain, place)
            send_low(step, chain, place, row_of(high, 1 - mid, core))
            send_low(step, chain, place, row_of(high, mid, 1 - core))

    def forward_mid(step, chain):
        for index in range(tall):
            source = high if index == 0 else along(ranked(index - 1))
            place = spot(source, 1 - mid, core)
            await_low(step, chain, place)
            send_low(step, chain, place, row_of(high, mid, 1 - core))

    def await_core(step, chain):
        for offset in range(tall):
            for mid_at in range(2):
                await_low(step, chain, spot((high + offset) % tall, mid_at, 1 - core))

    def send_tiles(high_at):
        inner = me % (4 * near)

        def send_tile(offset, carry):
            other = high_at * (4 * near) + (inner + offset) % (4 * near)
            pltpu.make_async_remote_copy(
                src_ref=owned.at[other],
                dst_ref=mirror.at[me],
                send_sem=tile_send,
                recv_sem=tile_recv.at[row],
                device_id=(other // near, other % near),
                device_id_type=MESH,
            ).start()
            return carry

        return send_tile

    def send_group(index):
        if index < 0:
            lax.fori_loop(1, 4 * near, send_tiles(high), 0)
        else:
            lax.fori_loop(0, 4 * near, send_tiles(along(ranked(index))), 0)

    def build(step, carry):
        source = (row + far - step) % far
        base = source * near
        group = mirror.at[pl.ds(base, near)]
        pltpu.make_async_copy(group, group, tile_recv.at[source]).wait()
        fill(source)
        return carry

    def fill(source):
        lanes = (source % 2) * chips + source // 2
        lanes = pl.ds(pl.multiple_of(lanes * tile, tile), tile)
        for near_at in range(near):
            index = source * near + near_at
            window[near_at * tile : (near_at + 1) * tile, lanes] = (
                owned[index] + mirror[index].T
            )

    def multiply(step, chain, near_at):
        total = jnp.zeros((tile, cut), jnp.float32)
        matrix = window[pl.ds(pl.multiple_of(near_at * tile, tile), tile), :]
        vectors = low[step, chain].reshape(far * tile, cut)
        return total + jnp.dot(matrix, vectors, preferred_element_type=jnp.float32)

    def product(step, chain):
        for offset in range(1, near):
            other = (col + offset) % near
            partial[step, chain, other] = multiply(step, chain, other)
            pltpu.make_async_remote_copy(
                src_ref=partial.at[step, chain, other],
                dst_ref=arrived.at[step, chain, col],
                send_sem=part_send.at[step, chain],
                recv_sem=part_recv.at[step, chain, col],
                device_id=(row, other),
                device_id_type=MESH,
            ).start()
        mine[chain] = multiply(step, chain, col) + jnp.dot(
            diagonal[...], low[step, chain, own_spot], preferred_element_type=jnp.float32
        )

    def finish(step, chain, sigma):
        total = mine[chain]
        for offset in range(1, near):
            other = (col + offset) % near
            here = arrived.at[step, chain, other]
            pltpu.make_async_copy(here, here, part_recv.at[step, chain, other]).wait()
            total = total + arrived[step, chain, other]
        where = columns(chain)
        current = start_ref[:, where] if step == 0 else state[step - 1, :, where]
        if step == 0:
            following = (total - center * current) * (sigma_one / half_width)
            sigma_next = sigma_one
        else:
            before = start_ref[:, where] if step == 1 else state[step - 2, :, where]
            sigma_next = 1.0 / (2.0 / sigma_one - sigma)
            following = (total - center * current) * (
                2.0 * sigma_next / half_width
            ) - (sigma * sigma_next) * before
        if step == DEGREE - 1:
            out_ref[:, where] = following
        else:
            low[step + 1, chain, own_spot] = following.astype(jnp.bfloat16)
            begin(step + 1, chain)
            state[step, :, where] = following
        return sigma_next

    for chain in range(CHAINS):
        begin(0, chain)
    groups = list(range(tall - 2, -2, -1))
    for index in groups:
        send_group(index)
    for chain in range(CHAINS):
        forward_line(0, chain)
    for chain in range(CHAINS):
        forward_mid(0, chain)

    if near > 1:
        group = mirror.at[pl.ds(row * near, near - 1)]
        pltpu.make_async_copy(group, group, tile_recv.at[row]).wait()
    fill(row)
    lax.fori_loop(1, far, build, 0)

    sigmas = [sigma_one] * CHAINS

    def phase(chain, index):
        step, part = index // 4, index % 4
        if part == 0:
            forward_line(step, chain)
        elif part == 1:
            forward_mid(step, chain)
        elif part == 2:
            await_core(step, chain)
            product(step, chain)
        else:
            sigmas[chain] = finish(step, chain, sigmas[chain])

    for index in range(2, 4 * DEGREE + LAG * (CHAINS - 1)):
        for chain in range(CHAINS):
            own_index = index - LAG * chain
            if 2 <= own_index < 4 * DEGREE:
                phase(chain, own_index)

    group = owned.at[pl.ds(0, count - 1)]
    pltpu.make_async_copy(group, group, tile_send).wait()
    for step in range(DEGREE):
        for chain in range(CHAINS):
            group = low.at[step, chain, pl.ds(0, far - 1)]
            pltpu.make_async_copy(group, group, low_send.at[step, chain]).wait()
            if near > 1:
                group = partial.at[step, chain, pl.ds(0, near - 1)]
                pltpu.make_async_copy(group, group, part_send.at[step, chain]).wait()


def local(start_block, tiles, tile_rows, tile_cols, bounds):
    tall, width = start_block.shape
    tile = tiles.shape[-1]
    slots = tiles.shape[2]
    far = lax.axis_size("row")
    near = lax.axis_size("col")
    assert tall == tile and far % 4 == 0
    count = far * near
    cut = width // CHAINS
    smem = pl.BlockSpec(memory_space=pltpu.SMEM)
    vmem = pl.BlockSpec(memory_space=pltpu.VMEM)
    return pl.pallas_call(
        functools.partial(kernel, far, near, slots, tile, width),
        out_shape=jax.ShapeDtypeStruct((tall, width), jnp.float32),
        in_specs=[smem, smem, smem, vmem, vmem],
        out_specs=vmem,
        scratch_shapes=[
            pltpu.VMEM((slots + 1, tile, tile), jnp.bfloat16),
            pltpu.VMEM((count, tile, tile), jnp.bfloat16),
            pltpu.VMEM((count, tile, tile), jnp.bfloat16),
            pltpu.VMEM((near * tile, far * tile), jnp.bfloat16),
            pltpu.VMEM((tile, tile), jnp.bfloat16),
            pltpu.VMEM((DEGREE, CHAINS, far, tile, cut), jnp.bfloat16),
            pltpu.VMEM((DEGREE, CHAINS, near, tile, cut), jnp.float32),
            pltpu.VMEM((DEGREE, CHAINS, near, tile, cut), jnp.float32),
            pltpu.VMEM((CHAINS, tile, cut), jnp.float32),
            pltpu.VMEM((DEGREE, tile, width), jnp.float32),
            pltpu.SemaphoreType.DMA(()),
            pltpu.SemaphoreType.DMA((far,)),
            pltpu.SemaphoreType.DMA((DEGREE, CHAINS)),
            pltpu.SemaphoreType.DMA((DEGREE, CHAINS, far)),
            pltpu.SemaphoreType.DMA((DEGREE, CHAINS)),
            pltpu.SemaphoreType.DMA((DEGREE, CHAINS, near)),
        ],
        compiler_params=pltpu.CompilerParams(
            collective_id=0, has_side_effects=True, vmem_limit_bytes=60 * 1024 * 1024
        ),
    )(
        tile_rows.reshape(slots),
        tile_cols.reshape(slots),
        bounds,
        start_block,
        tiles.reshape(slots, tile, tile),
    )


def solution(mesh):
    placed = (
        P(("row", "col"), None),
        P("row", "col", None, None, None),
        P("row", "col", None),
        P("row", "col", None),
        P(),
    )
    return jax.shard_map(
        local, mesh=mesh, in_specs=placed, out_specs=P(("row", "col"), None), check_vma=False
    )
```

profile of v0, /device:TPU:0, one launch (start us, length us, event | category | flops | bytes accessed | tf_op | source)
XLA Modules:
  0.0 87.6 jit_solution(5014590945389934610)
XLA Ops:
  0.0 86.0 %shard_map.55 = f32[128,256]{1,0:T(8,128)} custom-call(s32[14]{0:T(128)} %bitcast.4, s32[14]{0:T(128)} %bitcast.5, f32[3]{0:T(128)} %bounds_ref.1, f32[128,256]{1,0:T(8,128)} %start_ref.1, bf16[14,128,128]{2,1,0:T(8,128)(2,1)} %bitcast.3), custom_call_target="tpu_custom_call" | custom-call | tf_op jit(solution)/shard_map/pallas_call | solution.py:284
  86.1 1.6 %copy.7 = f32[128,256]{1,0:T(8,128)} copy(f32[128,256]{1,0:T(8,128)} %shard_map.55) | data formatting | bytes 262144
where the time goes:
time: 87.8 us; the launch traced here: 87.6 us
  Pallas kernels  86 us (98%)
  local copies, waits for them, and re-layouts  1.57 us (2%)
    pallas_call x1, Pallas kernels, local(): pl.pallas_call(functools.partial(kernel, far, near, slots, tile, width),...  86 us

commit v1 on v0

--- a/solution.py
+++ b/solution.py
@@ -1,4 +1,5 @@
 import functools
+import math
 
 import jax
 import jax.numpy as jnp
@@ -10,10 +11,12 @@
 DEGREE = 4
 CHAINS = 2
 LAG = 0
+PARTS = 2
+ROOM = 48 * 1024 * 1024
 MESH = pl.DeviceIdType.MESH
 
 
-def kernel(
+def wide_kernel(
     far, near, slots, tile, width,
     rows_ref, cols_ref, bounds_ref, start_ref, tiles_ref, out_ref,
     placed, owned, mirror, window, diagonal, low, partial, arrived, mine, state,
@@ -270,6 +273,449 @@
                 pltpu.make_async_copy(group, group, part_send.at[step, chain]).wait()
 
 
+def plane_kernel(
+    tall, near, slots, tile, width,
+    rows_ref, cols_ref, bounds_ref, start_ref, tiles_ref, out_ref,
+    placed, owned, direct, mirror, forward, backward, give, take, low,
+    part_out, part_in, mine, state, last, last_in,
+    near_tiles_send, far_tiles_send, core_tiles_send, core_far_send,
+    near_tiles_recv, far_tiles_recv, core_tiles_recv, core_far_recv,
+    give_send, give_recv, low_send, line_send, low_recv, line_recv,
+    part_send, back_send, part_recv, back_recv, last_send, last_recv,
+):
+    far = 4 * tall
+    count = far * near
+    plane = 2 * near
+    line = tall // 2
+    half = width // 2
+    cut = half // PARTS
+    pair = 2 * tile
+    row = lax.axis_index("row")
+    col = lax.axis_index("col")
+    core = row % 2
+    mid = row // 2 % 2
+    high = row // 4
+    here = mid * near + col
+
+    def device(high_at, mid_at, core_at, col_at):
+        return ((high_at * 2 + mid_at) * 2 + core_at, col_at)
+
+    def beside(offset):
+        other = (here + offset) % plane
+        return device(high, other // near, core, other % near)
+
+    partner = device(high, mid, 1 - core, col)
+
+    from_ok = [high != 2 * m for m in range(line)]
+    from_at = [
+        jnp.where(high < 2 * m, high + tall - 2 * m, high - 2 * m - 1) for m in range(line)
+    ]
+    into_ok = [high != tall - 1 - 2 * m for m in range(line)]
+    into_at = [
+        jnp.where(high >= tall - 2 * m, high - tall + 2 * m, high + 2 * m + 1)
+        for m in range(line)
+    ]
+
+    def copy(src, dst, send, recv, to):
+        pltpu.make_async_remote_copy(
+            src_ref=src, dst_ref=dst, send_sem=send, recv_sem=recv,
+            device_id=to, device_id_type=MESH,
+        ).start()
+
+    def wait(ref, sem):
+        pltpu.make_async_copy(ref, ref, sem).wait()
+
+    barrier = pltpu.get_barrier_semaphore()
+
+    def greet(step, carry):
+        other = (row // 2 * near + col + step) % (far // 2 * near)
+        pl.semaphore_signal(
+            barrier, inc=1, device_id=(other // near * 2 + core, other % near),
+            device_id_type=MESH,
+        )
+        return carry
+
+    lax.fori_loop(1, far // 2 * near, greet, 0)
+    pl.semaphore_signal(barrier, inc=1, device_id=partner, device_id_type=MESH)
+
+    span = (1, pair)
+    lowest = jnp.full(span, bounds_ref[0], jnp.float32)
+    lower = jnp.full(span, bounds_ref[1], jnp.float32)
+    upper = jnp.full(span, bounds_ref[2], jnp.float32)
+    half_width = (upper - lower) * 0.5
+    center = (upper + lower) * 0.5
+    sigma_one = half_width / (lowest - center)
+
+    def lanes(at, size):
+        return pl.ds(pl.multiple_of(at * size, size), size)
+
+    give[...] = start_ref[:, lanes(1 - core, half)].T
+    kept = start_ref[:, lanes(core, half)].T
+    for chain in range(PARTS):
+        state[0, chain, :, lanes(core, tile)] = kept[chain * cut : (chain + 1) * cut]
+
+    for slot in range(slots):
+        placed[slot] = tiles_ref[slot]
+    placed[slots] = jnp.zeros((tile, tile), jnp.bfloat16)
+    places = []
+    for slot in range(slots):
+        glob_row = rows_ref[slot]
+        glob_col = cols_ref[slot]
+        place = (glob_col // near) * near + (glob_row - row * near)
+        places.append(jnp.where(glob_row >= 0, place, -1))
+
+    def put(position, carry):
+        chosen = jnp.int32(slots)
+        for slot in range(slots):
+            chosen = jnp.where(places[slot] == position, slot, chosen)
+        owned[position // near, position % near] = placed[chosen]
+        return carry
+
+    lax.fori_loop(0, count, put, 0)
+
+    def owned_at(high_at, mid_at):
+        return pl.ds((high_at * 2 + mid_at) * 2, 2)
+
+    direct[0, mid, core] = owned[owned_at(high, mid)]
+    for m in range(line):
+
+        @pl.when(from_ok[m])
+        def _(m=m):
+            direct[1 + m, mid, core] = owned[owned_at(from_at[m], mid)]
+
+        @pl.when(jnp.logical_not(from_ok[m]))
+        def _(m=m):
+            forward[:, (1 + m) * pair : (2 + m) * pair] = jnp.zeros(
+                (plane * pair, pair), jnp.bfloat16
+            )
+            backward[(1 + m) * pair : (2 + m) * pair, :] = jnp.zeros(
+                (pair, plane * pair), jnp.bfloat16
+            )
+            for step in range(DEGREE):
+                for chain in range(PARTS):
+                    low[step, chain, plane + m] = jnp.zeros((cut, pair), jnp.bfloat16)
+
+        @pl.when(jnp.logical_not(into_ok[m]))
+        def _(m=m):
+            for step in range(DEGREE):
+                for chain in range(PARTS):
+                    part_in[step, chain, plane - 1 + m] = jnp.zeros((cut, pair), jnp.bfloat16)
+
+    pl.semaphore_wait(barrier, far // 2 * near)
+
+    copy(give, take, give_send, give_recv, partner)
+    for m in reversed(range(line)):
+
+        @pl.when(into_ok[m])
+        def _(m=m):
+            for offset in range(near):
+                other = (col + offset) % near
+                copy(
+                    owned.at[pl.ds(into_at[m] * 4, 4), other], mirror.at[m, core, col],
+                    far_tiles_send.at[m], far_tiles_recv.at[m, col],
+                    device(into_at[m], mid, core, other),
+                )
+
+    def each_slot(act):
+        act(0, high)
+        for m in range(line):
+
+            @pl.when(from_ok[m])
+            def _(m=m):
+                act(1 + m, from_at[m])
+
+    def send_near(slot, high_at):
+        copy(
+            owned.at[owned_at(high_at, 1 - mid)], direct.at[slot, mid, core],
+            near_tiles_send.at[slot], near_tiles_recv.at[slot],
+            device(high, 1 - mid, core, col),
+        )
+        copy(
+            owned.at[owned_at(high_at, mid)], direct.at[slot, mid, core],
+            core_tiles_send.at[slot, 0], core_tiles_recv.at[slot, 0], partner,
+        )
+
+    each_slot(send_near)
+
+    def begin(step, chain):
+        own = low.at[step, chain, 0]
+        for m in reversed(range(line)):
+
+            @pl.when(into_ok[m])
+            def _(m=m):
+                copy(
+                    own, low.at[step, chain, plane + m],
+                    line_send.at[step, chain, m], line_recv.at[step, chain, m],
+                    device(into_at[m], mid, core, col),
+                )
+
+        for offset in range(1, plane):
+            copy(
+                own, low.at[step, chain, plane - offset],
+                low_send.at[step, chain], low_recv.at[step, chain], beside(offset),
+            )
+
+    wait(take, give_recv)
+    for chain in range(PARTS):
+        state[0, chain, :, lanes(1 - core, tile)] = take[chain * cut : (chain + 1) * cut, :]
+        low[0, chain, 0] = state[0, chain].astype(jnp.bfloat16)
+        begin(0, chain)
+
+    def pass_near(slot, high_at):
+        block = direct.at[slot, 1 - mid, core]
+        wait(block, near_tiles_recv.at[slot])
+        copy(
+            block, block, core_tiles_send.at[slot, 1], core_tiles_recv.at[slot, 1], partner
+        )
+
+    each_slot(pass_near)
+
+    def pass_far(m, offset):
+        other = (col + offset) % near
+        block = mirror.at[m, core, other]
+        wait(block, far_tiles_recv.at[m, other])
+        copy(block, block, core_far_send.at[m, other], core_far_recv.at[m, other], partner)
+
+    for m in range(line):
+
+        @pl.when(from_ok[m])
+        def _(m=m):
+            for offset in range(near):
+                pass_far(m, offset)
+
+    def spots(index, slot):
+        mid_at = index // (4 * near)
+        core_at = index // (2 * near) % 2
+        other_core = index // near % 2
+        col_at = index % near
+        offset = (mid_at * near + col_at + plane - here) % plane
+        inner = pl.ds(pl.multiple_of((offset * 2 + core_at) * tile, tile), tile)
+        outer = pl.ds(pl.multiple_of((slot * 2 + other_core) * tile, tile), tile)
+        return mid_at, core_at, other_core, col_at, inner, outer
+
+    def fill_own(index, carry):
+        mid_at, core_at, other_core, col_at, inner, outer = spots(index, 0)
+        block = direct[0, mid_at, core_at, other_core, col_at]
+        forward[inner, outer] = block
+        backward[outer, inner] = block.T
+        return carry
+
+    def fill_far(m):
+        def fill(index, carry):
+            mid_at, core_at, other_core, col_at, inner, outer = spots(index, 1 + m)
+            block = direct[1 + m, mid_at, core_at, other_core, col_at]
+            other = mirror[m, other_core, col_at, mid_at * 2 + core_at]
+            forward[inner, outer] = block + other.T
+            backward[outer, inner] = block.T + other
+            return carry
+
+        return fill
+
+    def await_near(slot, high_at):
+        wait(direct.at[slot, mid, 1 - core], core_tiles_recv.at[slot, 0])
+        wait(direct.at[slot, 1 - mid, 1 - core], core_tiles_recv.at[slot, 1])
+
+    blocks = 8 * near
+    await_near(0, high)
+    lax.fori_loop(0, blocks, fill_own, 0)
+    for m in range(line):
+
+        @pl.when(from_ok[m])
+        def _(m=m):
+            await_near(1 + m, from_at[m])
+            for other in range(near):
+                wait(mirror.at[m, 1 - core, other], core_far_recv.at[m, other])
+            lax.fori_loop(0, blocks, fill_far(m), 0)
+
+    def product(step, chain):
+        wait(low.at[step, chain, pl.ds(1, plane - 1)], low_recv.at[step, chain])
+        total = jnp.zeros((cut, (1 + line) * pair), jnp.float32)
+        for offset in range(plane):
+            total = total + jnp.dot(
+                low[step, chain, offset], forward[offset * pair : (offset + 1) * pair, :],
+                preferred_element_type=jnp.float32,
+            )
+        kept = total[:, :pair]
+        for m in range(line):
+            at = plane - 1 + m
+            part_out[step, chain, at] = total[:, (1 + m) * pair : (2 + m) * pair].astype(
+                jnp.bfloat16
+            )
+        for m in reversed(range(line)):
+
+            @pl.when(from_ok[m])
+            def _(m=m):
+                at = plane - 1 + m
+                copy(
+                    part_out.at[step, chain, at], part_in.at[step, chain, at],
+                    back_send.at[step, chain, m], back_recv.at[step, chain, m],
+                    device(from_at[m], mid, core, col),
+                )
+
+        for m in range(line):
+
+            @pl.when(from_ok[m])
+            def _(m=m):
+                wait(low.at[step, chain, plane + m], line_recv.at[step, chain, m])
+
+        total = jnp.dot(
+            low[step, chain, 0], backward[:pair, :], preferred_element_type=jnp.float32
+        )
+        for m in range(line):
+            total = total + jnp.dot(
+                low[step, chain, plane + m], backward[(1 + m) * pair : (2 + m) * pair, :],
+                preferred_element_type=jnp.float32,
+            )
+        mine[chain] = kept + total[:, :pair]
+        for offset in range(1, plane):
+            part_out[step, chain, offset - 1] = total[
+                :, offset * pair : (offset + 1) * pair
+            ].astype(jnp.bfloat16)
+            copy(
+                part_out.at[step, chain, offset - 1],
+                part_in.at[step, chain, plane - offset - 1],
+                part_send.at[step, chain], part_recv.at[step, chain], beside(offset),
+            )
+
+    def finish(step, chain, sigma):
+        wait(part_in.at[step, chain, pl.ds(0, plane - 1)], part_recv.at[step, chain])
+        for m in range(line):
+
+            @pl.when(into_ok[m])
+            def _(m=m):
+                wait(part_in.at[step, chain, plane - 1 + m], back_recv.at[step, chain, m])
+
+        total = mine[chain]
+        for at in range(plane - 1 + line):
+            total = total + part_in[step, chain, at].astype(jnp.float32)
+        current = state[step, chain]
+        if step == 0:
+            sigma_next = sigma_one
+            following = (total - center * current) * (sigma_one / half_width)
+        else:
+            sigma_next = 1.0 / (2.0 / sigma_one - sigma)
+            following = (total - center * current) * (
+                2.0 * sigma_next / half_width
+            ) - (sigma * sigma_next) * state[step - 1, chain]
+        if step == DEGREE - 1:
+            last[chain] = following
+            copy(
+                last.at[chain, :, lanes(1 - core, tile)], last_in.at[chain],
+                last_send.at[chain], last_recv.at[chain], partner,
+            )
+        else:
+            low[step + 1, chain, 0] = following.astype(jnp.bfloat16)
+            begin(step + 1, chain)
+            state[step + 1, chain] = following
+        return sigma_next
+
+    sigmas = [sigma_one] * PARTS
+    for step in range(DEGREE):
+        for chain in range(PARTS):
+            product(step, chain)
+        for chain in range(PARTS):
+            sigmas[chain] = finish(step, chain, sigmas[chain])
+
+    own = last[:, :, lanes(core, tile)].reshape(half, tile)
+    out_ref[:, lanes(core, half)] = own.T
+    for chain in range(PARTS):
+        wait(last_in.at[chain], last_recv.at[chain])
+    out_ref[:, lanes(1 - core, half)] = last_in[...].reshape(half, tile).T
+
+    wait(give, give_send)
+    for chain in range(PARTS):
+        wait(last_in.at[chain], last_send.at[chain])
+
+    def close_near(slot, high_at):
+        block = direct.at[slot, mid, core]
+        wait(block, near_tiles_send.at[slot])
+        wait(block, core_tiles_send.at[slot, 0])
+        wait(block, core_tiles_send.at[slot, 1])
+
+    each_slot(close_near)
+    for m in range(line):
+
+        @pl.when(from_ok[m])
+        def _(m=m):
+            for other in range(near):
+                wait(mirror.at[m, core, other], core_far_send.at[m, other])
+            for step in range(DEGREE):
+                for chain in range(PARTS):
+                    wait(part_out.at[step, chain, plane - 1 + m], back_send.at[step, chain, m])
+
+        @pl.when(into_ok[m])
+        def _(m=m):
+            wait(mirror.at[m, core], far_tiles_send.at[m])
+            for step in range(DEGREE):
+                for chain in range(PARTS):
+                    wait(low.at[step, chain, 0], line_send.at[step, chain, m])
+
+    for step in range(DEGREE):
+        for chain in range(PARTS):
+            wait(low.at[step, chain, pl.ds(1, plane - 1)], low_send.at[step, chain])
+            wait(part_out.at[step, chain, pl.ds(0, plane - 1)], part_send.at[step, chain])
+
+
+def plane_scratch(tall, near, slots, tile, width):
+    far = 4 * tall
+    plane = 2 * near
+    line = tall // 2
+    half = width // 2
+    cut = half // PARTS
+    pair = 2 * tile
+    bf16, f32 = jnp.bfloat16, jnp.float32
+    memory = [
+        ((slots + 1, tile, tile), bf16),
+        ((far, near, tile, tile), bf16),
+        ((1 + line, 2, 2, 2, near, tile, tile), bf16),
+        ((line, 2, near, 4, tile, tile), bf16),
+        ((plane * pair, (1 + line) * pair), bf16),
+        (((1 + line) * pair, plane * pair), bf16),
+        ((half, tile), f32),
+        ((half, tile), f32),
+        ((DEGREE, PARTS, plane + line, cut, pair), bf16),
+        ((DEGREE, PARTS, plane - 1 + line, cut, pair), bf16),
+        ((DEGREE, PARTS, plane - 1 + line, cut, pair), bf16),
+        ((PARTS, cut, pair), f32),
+        ((DEGREE, PARTS, cut, pair), f32),
+        ((PARTS, cut, pair), f32),
+        ((PARTS, cut, tile), f32),
+    ]
+    chains = (DEGREE, PARTS)
+    semaphores = [
+        (1 + line,), (line,), (1 + line, 2), (line, near),
+        (1 + line,), (line, near), (1 + line, 2), (line, near),
+        (), (), chains, (*chains, line), chains, (*chains, line),
+        chains, (*chains, line), chains, (*chains, line), (PARTS,), (PARTS,),
+    ]
+    size = sum(math.prod(shape) * jnp.dtype(kind).itemsize for shape, kind in memory)
+    shapes = [pltpu.VMEM(shape, kind) for shape, kind in memory]
+    return size, shapes + [pltpu.SemaphoreType.DMA(shape) for shape in semaphores]
+
+
+def wide_scratch(far, near, slots, tile, width):
+    count = far * near
+    cut = width // CHAINS
+    return [
+        pltpu.VMEM((slots + 1, tile, tile), jnp.bfloat16),
+        pltpu.VMEM((count, tile, tile), jnp.bfloat16),
+        pltpu.VMEM((count, tile, tile), jnp.bfloat16),
+        pltpu.VMEM((near * tile, far * tile), jnp.bfloat16),
+        pltpu.VMEM((tile, tile), jnp.bfloat16),
+        pltpu.VMEM((DEGREE, CHAINS, far, tile, cut), jnp.bfloat16),
+        pltpu.VMEM((DEGREE, CHAINS, near, tile, cut), jnp.float32),
+        pltpu.VMEM((DEGREE, CHAINS, near, tile, cut), jnp.float32),
+        pltpu.VMEM((CHAINS, tile, cut), jnp.float32),
+        pltpu.VMEM((DEGREE, tile, width), jnp.float32),
+        pltpu.SemaphoreType.DMA(()),
+        pltpu.SemaphoreType.DMA((far,)),
+        pltpu.SemaphoreType.DMA((DEGREE, CHAINS)),
+        pltpu.SemaphoreType.DMA((DEGREE, CHAINS, far)),
+        pltpu.SemaphoreType.DMA((DEGREE, CHAINS)),
+        pltpu.SemaphoreType.DMA((DEGREE, CHAINS, near)),
+    ]
+
+
 def local(start_block, tiles, tile_rows, tile_cols, bounds):
     tall, width = start_block.shape
     tile = tiles.shape[-1]
@@ -277,33 +723,21 @@
     far = lax.axis_size("row")
     near = lax.axis_size("col")
     assert tall == tile and far % 4 == 0
-    count = far * near
-    cut = width // CHAINS
     smem = pl.BlockSpec(memory_space=pltpu.SMEM)
     vmem = pl.BlockSpec(memory_space=pltpu.VMEM)
+    body = functools.partial(wide_kernel, far, near, slots, tile, width)
+    scratch = wide_scratch(far, near, slots, tile, width)
+    if far % 8 == 0:
+        size, shapes = plane_scratch(far // 4, near, slots, tile, width)
+        if size <= ROOM:
+            body = functools.partial(plane_kernel, far // 4, near, slots, tile, width)
+            scratch = shapes
     return pl.pallas_call(
-        functools.partial(kernel, far, near, slots, tile, width),
+        body,
         out_shape=jax.ShapeDtypeStruct((tall, width), jnp.float32),
         in_specs=[smem, smem, smem, vmem, vmem],
         out_specs=vmem,
-        scratch_shapes=[
-            pltpu.VMEM((slots + 1, tile, tile), jnp.bfloat16),
-            pltpu.VMEM((count, tile, tile), jnp.bfloat16),
-            pltpu.VMEM((count, tile, tile), jnp.bfloat16),
-            pltpu.VMEM((near * tile, far * tile), jnp.bfloat16),
-            pltpu.VMEM((tile, tile), jnp.bfloat16),
-            pltpu.VMEM((DEGREE, CHAINS, far, tile, cut), jnp.bfloat16),
-            pltpu.VMEM((DEGREE, CHAINS, near, tile, cut), jnp.float32),
-            pltpu.VMEM((DEGREE, CHAINS, near, tile, cut), jnp.float32),
-            pltpu.VMEM((CHAINS, tile, cut), jnp.float32),
-            pltpu.VMEM((DEGREE, tile, width), jnp.float32),
-            pltpu.SemaphoreType.DMA(()),
-            pltpu.SemaphoreType.DMA((far,)),
-            pltpu.SemaphoreType.DMA((DEGREE, CHAINS)),
-            pltpu.SemaphoreType.DMA((DEGREE, CHAINS, far)),
-            pltpu.SemaphoreType.DMA((DEGREE, CHAINS)),
-            pltpu.SemaphoreType.DMA((DEGREE, CHAINS, near)),
-        ],
+        scratch_shapes=scratch,
         compiler_params=pltpu.CompilerParams(
             collective_id=0, has_side_effects=True, vmem_limit_bytes=60 * 1024 * 1024
         ),

time: 87.8 us -> 63.5 us (0.72)
  Pallas kernels: 86 us -> 61.8 us
    pallas_call x1, Pallas kernels: 86 us -> 61.8 us  [local(): pl.pallas_call(body, out_shape=jax.ShapeDtypeStruct((tall, width), jnp.fl...]
where the time goes in v1:
time: 63.5 us; the launch traced here: 63.3 us
  Pallas kernels  61.8 us (97%)
  local copies, waits for them, and re-layouts  1.57 us (2%)
    pallas_call x1, Pallas kernels, local(): pl.pallas_call(body, out_shape=jax.ShapeDtypeStruct((tall, width), jnp.fl...  61.8 us
    unnamed x1, local copies, waits for them, and re-layouts  1.57 us

profile of v1, /device:TPU:0, one launch (start us, length us, event | category | flops | bytes accessed | tf_op | source)
XLA Modules:
  0.0 63.3 jit_solution(7528992593624507965)
XLA Ops:
  0.0 61.8 %shard_map.55 = f32[128,256]{1,0:T(8,128)} custom-call(s32[14]{0:T(128)} %bitcast.4, s32[14]{0:T(128)} %bitcast.5, f32[3]{0:T(128)} %bounds_ref.1, f32[128,256]{1,0:T(8,128)} %start_ref.1, bf16[14,128,128]{2,1,0:T(8,128)(2,1)} %bitcast.3), custom_call_target="tpu_custom_call" | custom-call | tf_op jit(solution)/shard_map/pallas_call | solution.py:735
  61.8 1.6 %copy.7 = f32[128,256]{1,0:T(8,128)} copy(f32[128,256]{1,0:T(8,128)} %shard_map.55) | data formatting | bytes 262144

commit v2 on v1

--- a/solution.py
+++ b/solution.py
@@ -11,7 +11,7 @@
 DEGREE = 4
 CHAINS = 2
 LAG = 0
-PARTS = 2
+PARTS = 4
 ROOM = 48 * 1024 * 1024
 MESH = pl.DeviceIdType.MESH
 
@@ -277,7 +277,7 @@
     tall, near, slots, tile, width,
     rows_ref, cols_ref, bounds_ref, start_ref, tiles_ref, out_ref,
     placed, owned, direct, mirror, forward, backward, give, take, low,
-    part_out, part_in, mine, state, last, last_in,
+    part_out, part_in, mine, state, last, last_in, start, row_of, col_of, limits, load,
     near_tiles_send, far_tiles_send, core_tiles_send, core_far_send,
     near_tiles_recv, far_tiles_recv, core_tiles_recv, core_far_recv,
     give_send, give_recv, low_send, line_send, low_recv, line_recv,
@@ -338,10 +338,28 @@
     lax.fori_loop(1, far // 2 * near, greet, 0)
     pl.semaphore_signal(barrier, inc=1, device_id=partner, device_id_type=MESH)
 
+    loads = [
+        pltpu.make_async_copy(src, dst, load.at[index])
+        for index, (src, dst) in enumerate(
+            [
+                (rows_ref, row_of),
+                (cols_ref, col_of),
+                (bounds_ref, limits),
+                (start_ref, start),
+                (tiles_ref, placed.at[pl.ds(0, slots)]),
+            ]
+        )
+    ]
+    for item in loads:
+        item.start()
+    placed[slots] = jnp.zeros((tile, tile), jnp.bfloat16)
+    for item in loads[:4]:
+        item.wait()
+
     span = (1, pair)
-    lowest = jnp.full(span, bounds_ref[0], jnp.float32)
-    lower = jnp.full(span, bounds_ref[1], jnp.float32)
-    upper = jnp.full(span, bounds_ref[2], jnp.float32)
+    lowest = jnp.full(span, limits[0], jnp.float32)
+    lower = jnp.full(span, limits[1], jnp.float32)
+    upper = jnp.full(span, limits[2], jnp.float32)
     half_width = (upper - lower) * 0.5
     center = (upper + lower) * 0.5
     sigma_one = half_width / (lowest - center)
@@ -349,18 +367,15 @@
     def lanes(at, size):
         return pl.ds(pl.multiple_of(at * size, size), size)
 
-    give[...] = start_ref[:, lanes(1 - core, half)].T
-    kept = start_ref[:, lanes(core, half)].T
+    give[...] = start[:, lanes(1 - core, half)].T
+    kept = start[:, lanes(core, half)].T
     for chain in range(PARTS):
         state[0, chain, :, lanes(core, tile)] = kept[chain * cut : (chain + 1) * cut]
 
-    for slot in range(slots):
-        placed[slot] = tiles_ref[slot]
-    placed[slots] = jnp.zeros((tile, tile), jnp.bfloat16)
     places = []
     for slot in range(slots):
-        glob_row = rows_ref[slot]
-        glob_col = cols_ref[slot]
+        glob_row = row_of[slot]
+        glob_col = col_of[slot]
         place = (glob_col // near) * near + (glob_row - row * near)
         places.append(jnp.where(glob_row >= 0, place, -1))
 
@@ -371,6 +386,7 @@
         owned[position // near, position % near] = placed[chosen]
         return carry
 
+    loads[4].wait()
     lax.fori_loop(0, count, put, 0)
 
     def owned_at(high_at, mid_at):
@@ -418,7 +434,7 @@
 
     def each_slot(act):
         act(0, high)
-        for m in range(line):
+        for m in reversed(range(line)):
 
             @pl.when(from_ok[m])
             def _(m=m):
@@ -468,64 +484,77 @@
             block, block, core_tiles_send.at[slot, 1], core_tiles_recv.at[slot, 1], partner
         )
 
-    each_slot(pass_near)
-
     def pass_far(m, offset):
         other = (col + offset) % near
         block = mirror.at[m, core, other]
         wait(block, far_tiles_recv.at[m, other])
         copy(block, block, core_far_send.at[m, other], core_far_recv.at[m, other], partner)
 
-    for m in range(line):
-
-        @pl.when(from_ok[m])
-        def _(m=m):
-            for offset in range(near):
-                pass_far(m, offset)
-
-    def spots(index, slot):
-        mid_at = index // (4 * near)
-        core_at = index // (2 * near) % 2
-        other_core = index // near % 2
-        col_at = index % near
+    def spots(slot, mid_at, core_at, other_core, col_at):
         offset = (mid_at * near + col_at + plane - here) % plane
         inner = pl.ds(pl.multiple_of((offset * 2 + core_at) * tile, tile), tile)
         outer = pl.ds(pl.multiple_of((slot * 2 + other_core) * tile, tile), tile)
-        return mid_at, core_at, other_core, col_at, inner, outer
-
-    def fill_own(index, carry):
-        mid_at, core_at, other_core, col_at, inner, outer = spots(index, 0)
-        block = direct[0, mid_at, core_at, other_core, col_at]
-        forward[inner, outer] = block
-        backward[outer, inner] = block.T
-        return carry
-
-    def fill_far(m):
+        return inner, outer
+
+    def fill_near(slot, mid_at, core_at):
         def fill(index, carry):
-            mid_at, core_at, other_core, col_at, inner, outer = spots(index, 1 + m)
-            block = direct[1 + m, mid_at, core_at, other_core, col_at]
-            other = mirror[m, other_core, col_at, mid_at * 2 + core_at]
-            forward[inner, outer] = block + other.T
-            backward[outer, inner] = block.T + other
+            other_core, col_at = index // near, index % near
+            inner, outer = spots(slot, mid_at, core_at, other_core, col_at)
+            block = direct[slot, mid_at, core_at, other_core, col_at]
+            forward[inner, outer] = block
+            backward[outer, inner] = block.T
             return carry
 
-        return fill
-
-    def await_near(slot, high_at):
+        lax.fori_loop(0, 2 * near, fill, 0, unroll=2)
+
+    def fill_slot(slot, high_at):
+        fill_near(slot, mid, core)
+        fill_near(slot, 1 - mid, core)
         wait(direct.at[slot, mid, 1 - core], core_tiles_recv.at[slot, 0])
+        fill_near(slot, mid, 1 - core)
         wait(direct.at[slot, 1 - mid, 1 - core], core_tiles_recv.at[slot, 1])
-
-    blocks = 8 * near
-    await_near(0, high)
-    lax.fori_loop(0, blocks, fill_own, 0)
-    for m in range(line):
-
+        fill_near(slot, 1 - mid, 1 - core)
+
+    def fill_far(m, offset, other_core):
+        col_at = (col + offset) % near
+
+        def fill(index, carry):
+            inner, outer = spots(1 + m, index // 2, index % 2, other_core, col_at)
+            block = mirror[m, other_core, col_at, index]
+            forward[inner, outer] += block.T
+            backward[outer, inner] += block
+            return carry
+
+        lax.fori_loop(0, 4, fill, 0, unroll=2)
+
+    def fill_pair(m, offset):
+        fill_far(m, offset, core)
+        other = (col + offset) % near
+        wait(mirror.at[m, 1 - core, other], core_far_recv.at[m, other])
+        fill_far(m, offset, 1 - core)
+
+    def when_from(m, act):
         @pl.when(from_ok[m])
-        def _(m=m):
-            await_near(1 + m, from_at[m])
-            for other in range(near):
-                wait(mirror.at[m, 1 - core, other], core_far_recv.at[m, other])
-            lax.fori_loop(0, blocks, fill_far(m), 0)
+        def _():
+            act()
+
+    pass_near(0, high)
+    order = list(reversed(range(line)))
+    for place, m in enumerate(order):
+        for offset in range(near):
+            when_from(m, lambda m=m, offset=offset: pass_far(m, offset))
+            if offset == 0:
+                when_from(m, lambda m=m: pass_near(1 + m, from_at[m]))
+                if place == 0:
+                    fill_slot(0, high)
+        if place + 1 < line:
+            when_from(m, lambda m=m: fill_slot(1 + m, from_at[m]))
+            for offset in range(near):
+                when_from(m, lambda m=m, offset=offset: fill_pair(m, offset))
+        else:
+            when_from(m, lambda m=m: fill_slot(1 + m, from_at[m]))
+    for offset in range(near):
+        when_from(order[-1], lambda offset=offset: fill_pair(order[-1], offset))
 
     def product(step, chain):
         wait(low.at[step, chain, pl.ds(1, plane - 1)], low_recv.at[step, chain])
@@ -680,6 +709,7 @@
         ((DEGREE, PARTS, cut, pair), f32),
         ((PARTS, cut, pair), f32),
         ((PARTS, cut, tile), f32),
+        ((tile, width), f32),
     ]
     chains = (DEGREE, PARTS)
     semaphores = [
@@ -690,6 +720,12 @@
     ]
     size = sum(math.prod(shape) * jnp.dtype(kind).itemsize for shape, kind in memory)
     shapes = [pltpu.VMEM(shape, kind) for shape, kind in memory]
+    shapes += [
+        pltpu.SMEM((slots,), jnp.int32),
+        pltpu.SMEM((slots,), jnp.int32),
+        pltpu.SMEM((3,), jnp.float32),
+        pltpu.SemaphoreType.DMA((5,)),
+    ]
     return size, shapes + [pltpu.SemaphoreType.DMA(shape) for shape in semaphores]
 
 
@@ -727,15 +763,17 @@
     vmem = pl.BlockSpec(memory_space=pltpu.VMEM)
     body = functools.partial(wide_kernel, far, near, slots, tile, width)
     scratch = wide_scratch(far, near, slots, tile, width)
+    in_specs = [smem, smem, smem, vmem, vmem]
     if far % 8 == 0:
         size, shapes = plane_scratch(far // 4, near, slots, tile, width)
         if size <= ROOM:
             body = functools.partial(plane_kernel, far // 4, near, slots, tile, width)
             scratch = shapes
+            in_specs = [pl.BlockSpec(memory_space=pl.ANY)] * 5
     return pl.pallas_call(
         body,
         out_shape=jax.ShapeDtypeStruct((tall, width), jnp.float32),
-        in_specs=[smem, smem, smem, vmem, vmem],
+        in_specs=in_specs,
         out_specs=vmem,
         scratch_shapes=scratch,
         compiler_params=pltpu.CompilerParams(

time: 63.5 us -> 59.5 us (0.937)
  Pallas kernels: 61.8 us -> 57.8 us
    pallas_call x1, Pallas kernels: 61.8 us -> 57.8 us  [local(): pl.pallas_call(body, out_shape=jax.ShapeDtypeStruct((tall, width), jnp.fl...]
where the time goes in v2:
time: 59.5 us; the launch traced here: 59.4 us
  Pallas kernels  57.8 us (97%)
  local copies, waits for them, and re-layouts  1.57 us (3%)
    pallas_call x1, Pallas kernels, local(): pl.pallas_call(body, out_shape=jax.ShapeDtypeStruct((tall, width), jnp.fl...  57.8 us
    unnamed x1, local copies, waits for them, and re-layouts  1.57 us

profile of v2, /device:TPU:0, one launch (start us, length us, event | category | flops | bytes accessed | tf_op | source)
XLA Modules:
  0.0 59.4 jit_solution(2651812179306441749)
XLA Ops:
  0.0 57.8 %shard_map.55 = f32[128,256]{1,0:T(8,128)} custom-call(s32[14]{0:T(128)} %bitcast.4, s32[14]{0:T(128)} %bitcast.5, f32[3]{0:T(128)} %bounds_ref.1, f32[128,256]{1,0:T(8,128)} %start_ref.1, bf16[14,128,128]{2,1,0:T(8,128)(2,1)} %bitcast.3), custom_call_target="tpu_custom_call" | custom-call | tf_op jit(solution)/shard_map/pallas_call | solution.py:773
  57.8 1.6 %copy.7 = f32[128,256]{1,0:T(8,128)} copy(f32[128,256]{1,0:T(8,128)} %shard_map.55) | data formatting | bytes 262144

commit v3 on v2

--- a/solution.py
+++ b/solution.py
@@ -558,12 +558,8 @@
 
     def product(step, chain):
         wait(low.at[step, chain, pl.ds(1, plane - 1)], low_recv.at[step, chain])
-        total = jnp.zeros((cut, (1 + line) * pair), jnp.float32)
-        for offset in range(plane):
-            total = total + jnp.dot(
-                low[step, chain, offset], forward[offset * pair : (offset + 1) * pair, :],
-                preferred_element_type=jnp.float32,
-            )
+        vectors = jnp.concatenate([low[step, chain, at] for at in range(plane)], axis=1)
+        total = jnp.dot(vectors, forward[...], preferred_element_type=jnp.float32)
         kept = total[:, :pair]
         for m in range(line):
             at = plane - 1 + m
@@ -587,14 +583,10 @@
             def _(m=m):
                 wait(low.at[step, chain, plane + m], line_recv.at[step, chain, m])
 
-        total = jnp.dot(
-            low[step, chain, 0], backward[:pair, :], preferred_element_type=jnp.float32
+        vectors = jnp.concatenate(
+            [low[step, chain, at] for at in [0, *range(plane, plane + line)]], axis=1
         )
-        for m in range(line):
-            total = total + jnp.dot(
-                low[step, chain, plane + m], backward[(1 + m) * pair : (2 + m) * pair, :],
-                preferred_element_type=jnp.float32,
-            )
+        total = jnp.dot(vectors, backward[...], preferred_element_type=jnp.float32)
         mine[chain] = kept + total[:, :pair]
         for offset in range(1, plane):
             part_out[step, chain, offset - 1] = total[
@@ -772,7 +764,7 @@
             in_specs = [pl.BlockSpec(memory_space=pl.ANY)] * 5
     return pl.pallas_call(
         body,
-        out_shape=jax.ShapeDtypeStruct((tall, width), jnp.float32),
+        out_shape=pltpu.VMEM((tall, width), jnp.float32),
         in_specs=in_specs,
         out_specs=vmem,
         scratch_shapes=scratch,

time: 59.5 us -> 56.5 us (0.950)
  Pallas kernels: 57.8 us -> 55.7 us
  local copies, waits for them, and re-layouts: 1.57 us -> 0.66 us
    pallas_call x1, Pallas kernels: 57.8 us -> 55.7 us  [local(): pl.pallas_call(body, out_shape=pltpu.VMEM((tall, width), jnp.float32), in...]
    unnamed x1, local copies, waits for them, and re-layouts: 1.57 us -> 0.66 us
where the time goes in v3:
time: 56.5 us; the launch traced here: 56.3 us
  Pallas kernels  55.7 us (99%)
  local copies, waits for them, and re-layouts  0.66 us (1%)
    pallas_call x1, Pallas kernels, local(): pl.pallas_call(body, out_shape=pltpu.VMEM((tall, width), jnp.float32), in...  55.7 us

profile of v3, /device:TPU:0, one launch (start us, length us, event | category | flops | bytes accessed | tf_op | source)
XLA Modules:
  0.0 56.3 jit_solution(17444366136691794043)
XLA Ops:
  0.0 55.7 %shard_map.55 = f32[128,256]{1,0:T(8,128)S(1)} custom-call(s32[14]{0:T(128)} %bitcast.4, s32[14]{0:T(128)} %bitcast.5, f32[3]{0:T(128)} %bounds_ref.1, f32[128,256]{1,0:T(8,128)} %start_ref.1, bf16[14,128,128]{2,1,0:T(8,128)(2,1)} %bitcast.3), custom_call_target="tpu_custom_call" | custom-call | tf_op jit(solution)/shard_map/pallas_call | solution.py:765
  55.7 0.7 %copy.7 = f32[128,256]{1,0:T(8,128)} copy(f32[128,256]{1,0:T(8,128)S(1)} %shard_map.55) | data formatting | bytes 262144

commit v4 on v3

--- a/solution.py
+++ b/solution.py
@@ -284,7 +284,6 @@
     part_send, back_send, part_recv, back_recv, last_send, last_recv,
 ):
     far = 4 * tall
-    count = far * near
     plane = 2 * near
     line = tall // 2
     half = width // 2
@@ -295,14 +294,17 @@
     core = row % 2
     mid = row // 2 % 2
     high = row // 4
-    here = mid * near + col
 
     def device(high_at, mid_at, core_at, col_at):
         return ((high_at * 2 + mid_at) * 2 + core_at, col_at)
 
     def beside(offset):
-        other = (here + offset) % plane
-        return device(high, other // near, core, other % near)
+        return device(high, (mid + offset // near) % 2, core, (col + offset % near) % near)
+
+    def opposite(offset):
+        return offset // near * near + (near - offset % near) % near
+
+    offsets = list(reversed(range(1, plane)))
 
     partner = device(high, mid, 1 - core, col)
 
@@ -327,16 +329,15 @@
 
     barrier = pltpu.get_barrier_semaphore()
 
-    def greet(step, carry):
-        other = (row // 2 * near + col + step) % (far // 2 * near)
-        pl.semaphore_signal(
-            barrier, inc=1, device_id=(other // near * 2 + core, other % near),
-            device_id_type=MESH,
-        )
-        return carry
-
-    lax.fori_loop(1, far // 2 * near, greet, 0)
-    pl.semaphore_signal(barrier, inc=1, device_id=partner, device_id_type=MESH)
+    def greet(to):
+        pl.semaphore_signal(barrier, inc=1, device_id=to, device_id_type=MESH)
+
+    for step in reversed(range(1, tall)):
+        for offset in range(near):
+            greet(device((high + step) % tall, mid, core, (col + offset) % near))
+    for offset in offsets:
+        greet(beside(offset))
+    greet(partner)
 
     loads = [
         pltpu.make_async_copy(src, dst, load.at[index])
@@ -353,9 +354,85 @@
     for item in loads:
         item.start()
     placed[slots] = jnp.zeros((tile, tile), jnp.bfloat16)
-    for item in loads[:4]:
-        item.wait()
-
+    loads[0].wait()
+    loads[1].wait()
+
+    def lanes(at, size):
+        return pl.ds(pl.multiple_of(at * size, size), size)
+
+    places = []
+    for slot in range(slots):
+        glob_row = row_of[slot]
+        glob_col = col_of[slot]
+        place = (glob_col // near) * near + (glob_row - row * near)
+        places.append(jnp.where(glob_row >= 0, place, -1))
+
+    def pick(high_at):
+        def put(index, carry):
+            at, other = high_at * 4 + index // near, index % near
+            chosen = jnp.int32(slots)
+            for slot in range(slots):
+                chosen = jnp.where(places[slot] == at * near + other, slot, chosen)
+            owned[at, other] = placed[chosen]
+            return carry
+
+        lax.fori_loop(0, 4 * near, put, 0, unroll=4)
+
+    loads[4].wait()
+    for m in reversed(range(line)):
+
+        @pl.when(into_ok[m])
+        def _(m=m):
+            pick(into_at[m])
+
+    def owned_at(high_at, mid_at):
+        return pl.ds((high_at * 2 + mid_at) * 2, 2)
+
+    pl.semaphore_wait(barrier, (tall - 1) * near + plane)
+
+    for m in reversed(range(line)):
+
+        @pl.when(into_ok[m])
+        def _(m=m):
+            for offset in range(near):
+                other = (col + offset) % near
+                copy(
+                    owned.at[pl.ds(into_at[m] * 4, 4), other], mirror.at[m, core, col],
+                    far_tiles_send.at[m], far_tiles_recv.at[m, col],
+                    device(into_at[m], mid, core, other),
+                )
+
+    def each_slot(act):
+        act(0, high)
+        for m in reversed(range(line)):
+
+            @pl.when(from_ok[m])
+            def _(m=m):
+                act(1 + m, from_at[m])
+
+    def send_near(slot, high_at):
+        copy(
+            owned.at[owned_at(high_at, 1 - mid)], direct.at[slot, mid, core],
+            near_tiles_send.at[slot], near_tiles_recv.at[slot],
+            device(high, 1 - mid, core, col),
+        )
+        copy(
+            owned.at[owned_at(high_at, mid)], direct.at[slot, mid, core],
+            core_tiles_send.at[slot, 0], core_tiles_recv.at[slot, 0], partner,
+        )
+
+    each_slot(lambda slot, high_at: pick(high_at))
+    each_slot(send_near)
+
+    loads[3].wait()
+    give[...] = start[:, lanes(1 - core, half)].T
+    copy(give, take, give_send, give_recv, partner)
+    kept = start[:, lanes(core, half)].T
+    for chain in range(PARTS):
+        state[0, chain, :, lanes(core, tile)] = kept[chain * cut : (chain + 1) * cut]
+
+
+    loads[2].wait()
     span = (1, pair)
     lowest = jnp.full(span, limits[0], jnp.float32)
     lower = jnp.full(span, limits[1], jnp.float32)
@@ -364,33 +441,14 @@
     center = (upper + lower) * 0.5
     sigma_one = half_width / (lowest - center)
 
-    def lanes(at, size):
-        return pl.ds(pl.multiple_of(at * size, size), size)
-
-    give[...] = start[:, lanes(1 - core, half)].T
-    kept = start[:, lanes(core, half)].T
-    for chain in range(PARTS):
-        state[0, chain, :, lanes(core, tile)] = kept[chain * cut : (chain + 1) * cut]
-
-    places = []
-    for slot in range(slots):
-        glob_row = row_of[slot]
-        glob_col = col_of[slot]
-        place = (glob_col // near) * near + (glob_row - row * near)
-        places.append(jnp.where(glob_row >= 0, place, -1))
-
-    def put(position, carry):
-        chosen = jnp.int32(slots)
-        for slot in range(slots):
-            chosen = jnp.where(places[slot] == position, slot, chosen)
-        owned[position // near, position % near] = placed[chosen]
-        return carry
-
-    loads[4].wait()
-    lax.fori_loop(0, count, put, 0)
-
-    def owned_at(high_at, mid_at):
-        return pl.ds((high_at * 2 + mid_at) * 2, 2)
+    scales = [sigma_one / half_width]
+    shares = [None]
+    sigma = sigma_one
+    for step in range(1, DEGREE):
+        sigma_next = 1.0 / (2.0 / sigma_one - sigma)
+        scales.append(2.0 * sigma_next / half_width)
+        shares.append(sigma * sigma_next)
+        sigma = sigma_next
 
     direct[0, mid, core] = owned[owned_at(high, mid)]
     for m in range(line):
@@ -417,41 +475,6 @@
                 for chain in range(PARTS):
                     part_in[step, chain, plane - 1 + m] = jnp.zeros((cut, pair), jnp.bfloat16)
 
-    pl.semaphore_wait(barrier, far // 2 * near)
-
-    copy(give, take, give_send, give_recv, partner)
-    for m in reversed(range(line)):
-
-        @pl.when(into_ok[m])
-        def _(m=m):
-            for offset in range(near):
-                other = (col + offset) % near
-                copy(
-                    owned.at[pl.ds(into_at[m] * 4, 4), other], mirror.at[m, core, col],
-                    far_tiles_send.at[m], far_tiles_recv.at[m, col],
-                    device(into_at[m], mid, core, other),
-                )
-
-    def each_slot(act):
-        act(0, high)
-        for m in reversed(range(line)):
-
-            @pl.when(from_ok[m])
-            def _(m=m):
-                act(1 + m, from_at[m])
-
-    def send_near(slot, high_at):
-        copy(
-            owned.at[owned_at(high_at, 1 - mid)], direct.at[slot, mid, core],
-            near_tiles_send.at[slot], near_tiles_recv.at[slot],
-            device(high, 1 - mid, core, col),
-        )
-        copy(
-            owned.at[owned_at(high_at, mid)], direct.at[slot, mid, core],
-            core_tiles_send.at[slot, 0], core_tiles_recv.at[slot, 0], partner,
-        )
-
-    each_slot(send_near)
 
     def begin(step, chain):
         own = low.at[step, chain, 0]
@@ -465,9 +488,9 @@
                     device(into_at[m], mid, core, col),
                 )
 
-        for offset in range(1, plane):
+        for offset in offsets:
             copy(
-                own, low.at[step, chain, plane - offset],
+                own, low.at[step, chain, opposite(offset)],
                 low_send.at[step, chain], low_recv.at[step, chain], beside(offset),
             )
 
@@ -491,7 +514,7 @@
         copy(block, block, core_far_send.at[m, other], core_far_recv.at[m, other], partner)
 
     def spots(slot, mid_at, core_at, other_core, col_at):
-        offset = (mid_at * near + col_at + plane - here) % plane
+        offset = (mid_at + mid) % 2 * near + (col_at + near - col) % near
         inner = pl.ds(pl.multiple_of((offset * 2 + core_at) * tile, tile), tile)
         outer = pl.ds(pl.multiple_of((slot * 2 + other_core) * tile, tile), tile)
         return inner, outer
@@ -588,17 +611,17 @@
         )
         total = jnp.dot(vectors, backward[...], preferred_element_type=jnp.float32)
         mine[chain] = kept + total[:, :pair]
-        for offset in range(1, plane):
+        for offset in offsets:
             part_out[step, chain, offset - 1] = total[
                 :, offset * pair : (offset + 1) * pair
             ].astype(jnp.bfloat16)
             copy(
                 part_out.at[step, chain, offset - 1],
-                part_in.at[step, chain, plane - offset - 1],
+                part_in.at[step, chain, opposite(offset) - 1],
                 part_send.at[step, chain], part_recv.at[step, chain], beside(offset),
             )
 
-    def finish(step, chain, sigma):
+    def finish(step, chain):
         wait(part_in.at[step, chain, pl.ds(0, plane - 1)], part_recv.at[step, chain])
         for m in range(line):
 
@@ -610,14 +633,9 @@
         for at in range(plane - 1 + line):
             total = total + part_in[step, chain, at].astype(jnp.float32)
         current = state[step, chain]
-        if step == 0:
-            sigma_next = sigma_one
-            following = (total - center * current) * (sigma_one / half_width)
-        else:
-            sigma_next = 1.0 / (2.0 / sigma_one - sigma)
-            following = (total - center * current) * (
-                2.0 * sigma_next / half_width
-            ) - (sigma * sigma_next) * state[step - 1, chain]
+        following = (total - center * current) * scales[step]
+        if step > 0:
+            following = following - shares[step] * state[step - 1, chain]
         if step == DEGREE - 1:
             last[chain] = following
             copy(
@@ -628,14 +646,12 @@
             low[step + 1, chain, 0] = following.astype(jnp.bfloat16)
             begin(step + 1, chain)
             state[step + 1, chain] = following
-        return sigma_next
-
-    sigmas = [sigma_one] * PARTS
+
     for step in range(DEGREE):
         for chain in range(PARTS):
             product(step, chain)
         for chain in range(PARTS):
-            sigmas[chain] = finish(step, chain, sigmas[chain])
+            finish(step, chain)
 
     own = last[:, :, lanes(core, tile)].reshape(half, tile)
     out_ref[:, lanes(core, half)] = own.T

time: 56.5 us -> 55 us (0.973)
  Pallas kernels: 55.7 us -> 54.2 us
    pallas_call x1, Pallas kernels: 55.7 us -> 54.2 us  [local(): pl.pallas_call(body, out_shape=pltpu.VMEM((tall, width), jnp.float32), in...]
where the time goes in v4:
time: 55 us; the launch traced here: 54.8 us
  Pallas kernels  54.2 us (99%)
  local copies, waits for them, and re-layouts  0.66 us (1%)
    pallas_call x1, Pallas kernels, local(): pl.pallas_call(body, out_shape=pltpu.VMEM((tall, width), jnp.float32), in...  54.2 us

profile of v4, /device:TPU:0, one launch (start us, length us, event | category | flops | bytes accessed | tf_op | source)
XLA Modules:
  0.0 54.8 jit_solution(728657859401229199)
XLA Ops:
  0.0 54.2 %shard_map.55 = f32[128,256]{1,0:T(8,128)S(1)} custom-call(s32[14]{0:T(128)} %bitcast.4, s32[14]{0:T(128)} %bitcast.5, f32[3]{0:T(128)} %bounds_ref.1, f32[128,256]{1,0:T(8,128)} %start_ref.1, bf16[14,128,128]{2,1,0:T(8,128)(2,1)} %bitcast.3), custom_call_target="tpu_custom_call" | custom-call | tf_op jit(solution)/shard_map/pallas_call | solution.py:781
  54.2 0.7 %copy.7 = f32[128,256]{1,0:T(8,128)} copy(f32[128,256]{1,0:T(8,128)S(1)} %shard_map.55) | data formatting | bytes 262144

commit v5 on v4

--- a/solution.py
+++ b/solution.py
@@ -277,11 +277,12 @@
     tall, near, slots, tile, width,
     rows_ref, cols_ref, bounds_ref, start_ref, tiles_ref, out_ref,
     placed, owned, direct, mirror, forward, backward, give, take, low,
-    part_out, part_in, mine, state, last, last_in, start, row_of, col_of, limits, load,
+    part_out, part_in, mine, state, last, end_in, mine_in, peer, start, row_of, col_of, limits, load,
     near_tiles_send, far_tiles_send, core_tiles_send, core_far_send,
     near_tiles_recv, far_tiles_recv, core_tiles_recv, core_far_recv,
     give_send, give_recv, low_send, line_send, low_recv, line_recv,
-    part_send, back_send, part_recv, back_recv, last_send, last_recv,
+    part_send, back_send, part_recv, back_recv,
+    end_recv, end_back_recv, mine_send, mine_recv, peer_send, peer_recv,
 ):
     far = 4 * tall
     plane = 2 * near
@@ -298,8 +299,8 @@
     def device(high_at, mid_at, core_at, col_at):
         return ((high_at * 2 + mid_at) * 2 + core_at, col_at)
 
-    def beside(offset):
-        return device(high, (mid + offset // near) % 2, core, (col + offset % near) % near)
+    def beside(offset, core_at=core):
+        return device(high, (mid + offset // near) % 2, core_at, (col + offset % near) % near)
 
     def opposite(offset):
         return offset // near * near + (near - offset % near) % near
@@ -326,18 +327,6 @@
 
     def wait(ref, sem):
         pltpu.make_async_copy(ref, ref, sem).wait()
-
-    barrier = pltpu.get_barrier_semaphore()
-
-    def greet(to):
-        pl.semaphore_signal(barrier, inc=1, device_id=to, device_id_type=MESH)
-
-    for step in reversed(range(1, tall)):
-        for offset in range(near):
-            greet(device((high + step) % tall, mid, core, (col + offset) % near))
-    for offset in offsets:
-        greet(beside(offset))
-    greet(partner)
 
     loads = [
         pltpu.make_async_copy(src, dst, load.at[index])
@@ -353,6 +342,19 @@
     ]
     for item in loads:
         item.start()
+
+    barrier = pltpu.get_barrier_semaphore()
+
+    def greet(to):
+        pl.semaphore_signal(barrier, inc=1, device_id=to, device_id_type=MESH)
+
+    for step in reversed(range(1, tall)):
+        for offset in range(near):
+            greet(device((high + step) % tall, mid, core, (col + offset) % near))
+    for offset in offsets:
+        greet(beside(offset))
+    greet(partner)
+
     placed[slots] = jnp.zeros((tile, tile), jnp.bfloat16)
     loads[0].wait()
     loads[1].wait()
@@ -379,21 +381,23 @@
         lax.fori_loop(0, 4 * near, put, 0, unroll=4)
 
     loads[4].wait()
-    for m in reversed(range(line)):
+    targets = list(reversed(range(line)))
+
+    @pl.when(into_ok[targets[0]])
+    def _():
+        pick(into_at[targets[0]])
+
+    def owned_at(high_at, mid_at):
+        return pl.ds((high_at * 2 + mid_at) * 2, 2)
+
+    pl.semaphore_wait(barrier, (tall - 1) * near + plane)
+
+    for m in targets:
 
         @pl.when(into_ok[m])
         def _(m=m):
-            pick(into_at[m])
-
-    def owned_at(high_at, mid_at):
-        return pl.ds((high_at * 2 + mid_at) * 2, 2)
-
-    pl.semaphore_wait(barrier, (tall - 1) * near + plane)
-
-    for m in reversed(range(line)):
-
-        @pl.when(into_ok[m])
-        def _(m=m):
+            if m != targets[0]:
+                pick(into_at[m])
             for offset in range(near):
                 other = (col + offset) % near
                 copy(
@@ -471,9 +475,11 @@
 
         @pl.when(jnp.logical_not(into_ok[m]))
         def _(m=m):
-            for step in range(DEGREE):
-                for chain in range(PARTS):
+            for chain in range(PARTS):
+                for step in range(DEGREE - 1):
                     part_in[step, chain, plane - 1 + m] = jnp.zeros((cut, pair), jnp.bfloat16)
+                for other in range(2):
+                    end_in[chain, other, plane - 1 + m] = jnp.zeros((cut, tile), jnp.bfloat16)
 
 
     def begin(step, chain):
@@ -594,11 +600,20 @@
             @pl.when(from_ok[m])
             def _(m=m):
                 at = plane - 1 + m
-                copy(
-                    part_out.at[step, chain, at], part_in.at[step, chain, at],
-                    back_send.at[step, chain, m], back_recv.at[step, chain, m],
-                    device(from_at[m], mid, core, col),
-                )
+                if step < DEGREE - 1:
+                    copy(
+                        part_out.at[step, chain, at], part_in.at[step, chain, at],
+                        back_send.at[step, chain, m], back_recv.at[step, chain, m],
+                        device(from_at[m], mid, core, col),
+                    )
+                    return
+                for owner in (core, 1 - core):
+                    copy(
+                        part_out.at[step, chain, at, :, lanes(owner, tile)],
+                        end_in.at[chain, core, at],
+                        back_send.at[step, chain, m], end_back_recv.at[chain, core, m],
+                        device(from_at[m], mid, owner, col),
+                    )
 
         for m in range(line):
 
@@ -615,10 +630,24 @@
             part_out[step, chain, offset - 1] = total[
                 :, offset * pair : (offset + 1) * pair
             ].astype(jnp.bfloat16)
+            if step < DEGREE - 1:
+                copy(
+                    part_out.at[step, chain, offset - 1],
+                    part_in.at[step, chain, opposite(offset) - 1],
+                    part_send.at[step, chain], part_recv.at[step, chain], beside(offset),
+                )
+                continue
+            for owner in (core, 1 - core):
+                copy(
+                    part_out.at[step, chain, offset - 1, :, lanes(owner, tile)],
+                    end_in.at[chain, core, opposite(offset) - 1],
+                    part_send.at[step, chain], end_recv.at[chain, core],
+                    beside(offset, owner),
+                )
+        if step == DEGREE - 1:
             copy(
-                part_out.at[step, chain, offset - 1],
-                part_in.at[step, chain, opposite(offset) - 1],
-                part_send.at[step, chain], part_recv.at[step, chain], beside(offset),
+                mine.at[chain, :, lanes(1 - core, tile)], mine_in.at[chain],
+                mine_send.at[chain], mine_recv.at[chain], partner,
             )
 
     def finish(step, chain):
@@ -636,32 +665,41 @@
         following = (total - center * current) * scales[step]
         if step > 0:
             following = following - shares[step] * state[step - 1, chain]
-        if step == DEGREE - 1:
-            last[chain] = following
+        low[step + 1, chain, 0] = following.astype(jnp.bfloat16)
+        begin(step + 1, chain)
+        state[step + 1, chain] = following
+        if step + 1 >= DEGREE - 2:
+            at = step + 3 - DEGREE
             copy(
-                last.at[chain, :, lanes(1 - core, tile)], last_in.at[chain],
-                last_send.at[chain], last_recv.at[chain], partner,
+                state.at[step + 1, chain, :, lanes(1 - core, tile)], peer.at[at, chain],
+                peer_send.at[at, chain], peer_recv.at[at, chain], partner,
             )
+
+    def end(chain, owned_half):
+        half_at = core if owned_half else 1 - core
+        wait(end_in.at[chain, half_at, pl.ds(0, plane - 1)], end_recv.at[chain, half_at])
+        for m in range(line):
+
+            @pl.when(into_ok[m])
+            def _(m=m):
+                wait(end_in.at[chain, half_at, plane - 1 + m], end_back_recv.at[chain, half_at, m])
+
+        if owned_half:
+            where = lanes(core, tile)
+            total = mine[chain, :, where]
+            current = state[DEGREE - 1, chain, :, where]
+            before = state[DEGREE - 2, chain, :, where]
         else:
-            low[step + 1, chain, 0] = following.astype(jnp.bfloat16)
-            begin(step + 1, chain)
-            state[step + 1, chain] = following
-
-    for step in range(DEGREE):
-        for chain in range(PARTS):
-            product(step, chain)
-        for chain in range(PARTS):
-            finish(step, chain)
-
-    own = last[:, :, lanes(core, tile)].reshape(half, tile)
-    out_ref[:, lanes(core, half)] = own.T
-    for chain in range(PARTS):
-        wait(last_in.at[chain], last_recv.at[chain])
-    out_ref[:, lanes(1 - core, half)] = last_in[...].reshape(half, tile).T
-
-    wait(give, give_send)
-    for chain in range(PARTS):
-        wait(last_in.at[chain], last_send.at[chain])
+            wait(mine_in.at[chain], mine_recv.at[chain])
+            for at in range(2):
+                wait(peer.at[at, chain], peer_recv.at[at, chain])
+            total = mine_in[chain]
+            current = peer[1, chain]
+            before = peer[0, chain]
+        for at in range(plane - 1 + line):
+            total = total + end_in[chain, half_at, at].astype(jnp.float32)
+        following = (total - center[:, :tile] * current) * scales[DEGREE - 1][:, :tile]
+        last[0 if owned_half else 1, chain] = following - shares[DEGREE - 1][:, :tile] * before
 
     def close_near(slot, high_at):
         block = direct.at[slot, mid, core]
@@ -669,28 +707,62 @@
         wait(block, core_tiles_send.at[slot, 0])
         wait(block, core_tiles_send.at[slot, 1])
 
-    each_slot(close_near)
-    for m in range(line):
-
-        @pl.when(from_ok[m])
-        def _(m=m):
-            for other in range(near):
-                wait(mirror.at[m, core, other], core_far_send.at[m, other])
-            for step in range(DEGREE):
-                for chain in range(PARTS):
-                    wait(part_out.at[step, chain, plane - 1 + m], back_send.at[step, chain, m])
-
-        @pl.when(into_ok[m])
-        def _(m=m):
-            wait(mirror.at[m, core], far_tiles_send.at[m])
-            for step in range(DEGREE):
-                for chain in range(PARTS):
-                    wait(low.at[step, chain, 0], line_send.at[step, chain, m])
+    def close_tiles():
+        wait(give, give_send)
+        each_slot(close_near)
+        for m in range(line):
+
+            @pl.when(from_ok[m])
+            def _(m=m):
+                for other in range(near):
+                    wait(mirror.at[m, core, other], core_far_send.at[m, other])
+
+            @pl.when(into_ok[m])
+            def _(m=m):
+                wait(mirror.at[m, core], far_tiles_send.at[m])
+
+    def close_steps(steps):
+        for m in range(line):
+
+            @pl.when(from_ok[m])
+            def _(m=m):
+                for step in steps:
+                    for chain in range(PARTS):
+                        at = plane - 1 + m
+                        wait(part_out.at[step, chain, at], back_send.at[step, chain, m])
+
+            @pl.when(into_ok[m])
+            def _(m=m):
+                for step in steps:
+                    for chain in range(PARTS):
+                        wait(low.at[step, chain, 0], line_send.at[step, chain, m])
+
+        for step in steps:
+            for chain in range(PARTS):
+                wait(low.at[step, chain, pl.ds(1, plane - 1)], low_send.at[step, chain])
+                wait(part_out.at[step, chain, pl.ds(0, plane - 1)], part_send.at[step, chain])
 
     for step in range(DEGREE):
         for chain in range(PARTS):
-            wait(low.at[step, chain, pl.ds(1, plane - 1)], low_send.at[step, chain])
-            wait(part_out.at[step, chain, pl.ds(0, plane - 1)], part_send.at[step, chain])
+            product(step, chain)
+        if step == DEGREE - 1:
+            close_tiles()
+            close_steps(range(step))
+            for chain in range(PARTS):
+                end(chain, True)
+                end(chain, False)
+            break
+        for chain in range(PARTS):
+            finish(step, chain)
+
+    out_ref[:, lanes(core, half)] = last[0].reshape(half, tile).T
+    out_ref[:, lanes(1 - core, half)] = last[1].reshape(half, tile).T
+
+    for chain in range(PARTS):
+        wait(mine_in.at[chain], mine_send.at[chain])
+        for at in range(2):
+            wait(peer.at[at, chain], peer_send.at[at, chain])
+    close_steps([DEGREE - 1])
 
 
 def plane_scratch(tall, near, slots, tile, width):
@@ -715,8 +787,10 @@
         ((DEGREE, PARTS, plane - 1 + line, cut, pair), bf16),
         ((PARTS, cut, pair), f32),
         ((DEGREE, PARTS, cut, pair), f32),
-        ((PARTS, cut, pair), f32),
+        ((2, PARTS, cut, tile), f32),
+        ((PARTS, 2, plane - 1 + line, cut, tile), bf16),
         ((PARTS, cut, tile), f32),
+        ((2, PARTS, cut, tile), f32),
         ((tile, width), f32),
     ]
     chains = (DEGREE, PARTS)
@@ -724,7 +798,8 @@
         (1 + line,), (line,), (1 + line, 2), (line, near),
         (1 + line,), (line, near), (1 + line, 2), (line, near),
         (), (), chains, (*chains, line), chains, (*chains, line),
-        chains, (*chains, line), chains, (*chains, line), (PARTS,), (PARTS,),
+        chains, (*chains, line), chains, (*chains, line),
+        (PARTS, 2), (PARTS, 2, line), (PARTS,), (PARTS,), (2, PARTS), (2, PARTS),
     ]
     size = sum(math.prod(shape) * jnp.dtype(kind).itemsize for shape, kind in memory)
     shapes = [pltpu.VMEM(shape, kind) for shape, kind in memory]

time: 55 us -> 54.6 us (level)
  no operation moved by 1% of the time
where the time goes in v5:
time: 54.6 us; the launch traced here: 54.4 us
  Pallas kernels  53.8 us (99%)
  local copies, waits for them, and re-layouts  0.66 us (1%)
    pallas_call x1, Pallas kernels, local(): pl.pallas_call(body, out_shape=pltpu.VMEM((tall, width), jnp.float32), in...  53.8 us

profile of v5, /device:TPU:0, one launch (start us, length us, event | category | flops | bytes accessed | tf_op | source)
XLA Modules:
  0.0 54.4 jit_solution(3408326505484412054)
XLA Ops:
  0.0 53.8 %shard_map.55 = f32[128,256]{1,0:T(8,128)S(1)} custom-call(s32[14]{0:T(128)} %bitcast.4, s32[14]{0:T(128)} %bitcast.5, f32[3]{0:T(128)} %bounds_ref.1, f32[128,256]{1,0:T(8,128)} %start_ref.1, bf16[14,128,128]{2,1,0:T(8,128)(2,1)} %bitcast.3), custom_call_target="tpu_custom_call" | custom-call | tf_op jit(solution)/shard_map/pallas_call | solution.py:856
  53.8 0.7 %copy.7 = f32[128,256]{1,0:T(8,128)} copy(f32[128,256]{1,0:T(8,128)S(1)} %shard_map.55) | data formatting | bytes 262144

commit v6 on v5

--- a/solution.py
+++ b/solution.py
@@ -534,7 +534,7 @@
             backward[outer, inner] = block.T
             return carry
 
-        lax.fori_loop(0, 2 * near, fill, 0, unroll=2)
+        lax.fori_loop(0, 2 * near, fill, 0, unroll=4)
 
     def fill_slot(slot, high_at):
         fill_near(slot, mid, core)
@@ -554,7 +554,7 @@
             backward[outer, inner] += block
             return carry
 
-        lax.fori_loop(0, 4, fill, 0, unroll=2)
+        lax.fori_loop(0, 4, fill, 0, unroll=4)
 
     def fill_pair(m, offset):
         fill_far(m, offset, core)

time: 54.6 us -> 54 us (0.989)
  Pallas kernels: 53.8 us -> 53.2 us
    pallas_call x1, Pallas kernels: 53.8 us -> 53.2 us  [local(): pl.pallas_call(body, out_shape=pltpu.VMEM((tall, width), jnp.float32), in...]
where the time goes in v6:
time: 54 us; the launch traced here: 53.8 us
  Pallas kernels  53.2 us (99%)
  local copies, waits for them, and re-layouts  0.66 us (1%)
    pallas_call x1, Pallas kernels, local(): pl.pallas_call(body, out_shape=pltpu.VMEM((tall, width), jnp.float32), in...  53.2 us

profile of v6, /device:TPU:0, one launch (start us, length us, event | category | flops | bytes accessed | tf_op | source)
XLA Modules:
  0.0 53.8 jit_solution(4498414388963836263)
XLA Ops:
  0.0 53.2 %shard_map.55 = f32[128,256]{1,0:T(8,128)S(1)} custom-call(s32[14]{0:T(128)} %bitcast.4, s32[14]{0:T(128)} %bitcast.5, f32[3]{0:T(128)} %bounds_ref.1, f32[128,256]{1,0:T(8,128)} %start_ref.1, bf16[14,128,128]{2,1,0:T(8,128)(2,1)} %bitcast.3), custom_call_target="tpu_custom_call" | custom-call | tf_op jit(solution)/shard_map/pallas_call | solution.py:856
  53.2 0.7 %copy.7 = f32[128,256]{1,0:T(8,128)} copy(f32[128,256]{1,0:T(8,128)S(1)} %shard_map.55) | data formatting | bytes 262144

commit v7 on v6

--- a/solution.py
+++ b/solution.py
@@ -750,12 +750,13 @@
             close_steps(range(step))
             for chain in range(PARTS):
                 end(chain, True)
+            out_ref[:, lanes(core, half)] = last[0].reshape(half, tile).T
+            for chain in range(PARTS):
                 end(chain, False)
             break
         for chain in range(PARTS):
             finish(step, chain)
 
-    out_ref[:, lanes(core, half)] = last[0].reshape(half, tile).T
     out_ref[:, lanes(1 - core, half)] = last[1].reshape(half, tile).T
 
     for chain in range(PARTS):

time: 54 us -> 54.2 us (level)
  no operation moved by 1% of the time
where the time goes in v7:
time: 54.2 us; the launch traced here: 54 us
  Pallas kernels  53.3 us (98%)
  local copies, waits for them, and re-layouts  0.66 us (1%)
    pallas_call x1, Pallas kernels, local(): pl.pallas_call(body, out_shape=pltpu.VMEM((tall, width), jnp.float32), in...  53.3 us

profile of v7, /device:TPU:0, one launch (start us, length us, event | category | flops | bytes accessed | tf_op | source)
XLA Modules:
  0.0 54.0 jit_solution(2513745979258283232)
XLA Ops:
  0.0 53.3 %shard_map.55 = f32[128,256]{1,0:T(8,128)S(1)} custom-call(s32[14]{0:T(128)} %bitcast.4, s32[14]{0:T(128)} %bitcast.5, f32[3]{0:T(128)} %bounds_ref.1, f32[128,256]{1,0:T(8,128)} %start_ref.1, bf16[14,128,128]{2,1,0:T(8,128)(2,1)} %bitcast.3), custom_call_target="tpu_custom_call" | custom-call | tf_op jit(solution)/shard_map/pallas_call | solution.py:857
  53.3 0.7 %copy.7 = f32[128,256]{1,0:T(8,128)} copy(f32[128,256]{1,0:T(8,128)S(1)} %shard_map.55) | data formatting | bytes 262144
